TPU v7x, 32 devices: a whole 2x2x4 slice. The times are simulated.
32 devices in a mesh: row: 8 (over z, x), col: 4 (over y, core).
Axes of the slice: x: 2, y: 2, z: 4, core: 2. Of those that a mesh axis runs over, the one named last changes fastest.
Arguments:
- right_side: float32 [6, 8, 64, 128], P(None, 'row'), may hold values from -6 to 6
- inverses: float32 [6, 8, 128, 128], P(None, 'row'), may hold values from -1 to 3
- factor_blocks: bfloat16 [15, 8, 8, 128, 128], P(None, 'row', 'col'), may hold values from -0.15625 to 0.15625
- pattern: int32 [15, 8, 8], P(None, 'row', 'col'), may hold values 0 or 1
Outputs:
- forward_part: float32 [6, 8, 64, 128], P(None, 'row')
- solution: float32 [6, 8, 64, 128], P(None, 'row')
All inputs are finite; a program needn't handle non-finite values. No bound on the sum of `pattern` on one device may be relied on, other than what follows from the above.
Results may differ from a plain program's by a relative error of at most 0.014.
Values may be sent and summed in bfloat16 or wider, within the bound.
No kernel may reach another device: no remote copies, remote signals or barrier semaphores. Data moves between devices by JAX's collectives and lax.ppermute only.
A program may use at most 64 MiB of HBM per device.

v0:
```python
import jax
import jax.numpy as jnp
from jax import lax
from jax.sharding import PartitionSpec as P


def spread(block, axis, holder):
    block = jnp.where(lax.axis_index(axis) == holder, block, jnp.zeros_like(block))
    return lax.psum(block, axis)


def pair_number(higher, lower_level):
    return higher * (higher - 1) // 2 + lower_level


def masked_block(factor_blocks, pattern, pair_index):
    return jnp.where(
        pattern[pair_index][:, :, None, None] != 0,
        factor_blocks[pair_index],
        jnp.zeros((), factor_blocks.dtype),
    )


def shards(right_side, inverses, factor_blocks, pattern):
    levels = right_side.shape[0]
    width_col = factor_blocks.shape[2]
    row_index = lax.axis_index("row")
    col_index = lax.axis_index("col")
    solved = []
    gathered = []
    for height in range(levels):
        remaining = right_side[height]
        if height > 0:
            partial_value = jnp.zeros(remaining.shape, jnp.float32)
            for earlier in range(height):
                masked = masked_block(factor_blocks, pattern, pair_number(height, earlier))
                partial_value = partial_value + jnp.einsum(
                    "ikab,knb->ina", masked, gathered[earlier], preferred_element_type=jnp.float32
                )
            summed = lax.psum(partial_value.astype(jnp.bfloat16), "col").astype(jnp.float32)
            remaining = remaining - summed
        segment = jnp.einsum(
            "inb,iab->ina", remaining, inverses[height], precision=lax.Precision.HIGHEST
        )
        solved.append(segment)
        if height < levels - 1:
            gathered_all = lax.all_gather(segment.astype(jnp.bfloat16), "row", axis=0, tiled=True)
            gathered.append(
                lax.dynamic_slice_in_dim(gathered_all, col_index * width_col, width_col, 0)
            )
    results = [None] * levels
    settled = [None] * levels
    for height in range(levels - 1, -1, -1):
        remaining = solved[height]
        if height < levels - 1:
            partial_value = jnp.zeros((width_col,) + remaining.shape[1:], jnp.float32)
            for later in range(height + 1, levels):
                masked = masked_block(factor_blocks, pattern, pair_number(later, height))
                partial_value = partial_value + jnp.einsum(
                    "ikab,ina->knb", masked, settled[later], preferred_element_type=jnp.float32
                )
            offset = jnp.clip(row_index - col_index * width_col, 0, width_col - 1)
            owner_col = row_index // width_col
            summed = lax.psum(partial_value, "row")
            own_sum = lax.dynamic_slice_in_dim(summed, offset, 1, 0)
            own_sum = spread(own_sum.astype(jnp.bfloat16), "col", owner_col).astype(own_sum.dtype)
            remaining = remaining - own_sum
        segment = jnp.einsum(
            "ina,iab->inb", remaining, inverses[height], precision=lax.Precision.HIGHEST
        )
        results[height] = segment
        settled[height] = segment.astype(jnp.bfloat16)
    return (jnp.stack(solved), jnp.stack(results))


def solution(mesh):
    placed = (
        P(None, "row", None, None),
        P(None, "row", None, None),
        P(None, "row", "col", None, None),
        P(None, "row", "col"),
    )
    return jax.shard_map(
        shards,
        mesh=mesh,
        in_specs=placed,
        out_specs=(P(None, "row", None, None), P(None, "row", None, None)),
        check_vma=False,
    )
```

profile of v0, /device:TPU:0, one launch (start us, length us, event | category | flops | bytes accessed | tf_op | source)
XLA Modules:
  0.0 446.8 jit_solution(956539431709333284)
XLA Ops:
  0.7 1.7 compare_reduce_fusion
  2.3 1.1 bitcast_dynamic-update-slice_fusion.10
  3.5 32.3 %all-gather = bf16[512,128]{1,0:T(8,128)(2,1)S(1)} all-gather(bf16[64,128]{1,0:T(8,128)(2,1)S(1)} %convert_element_type.125), channel_id=2, replica_groups=mesh['row'=8,'col'=4] {'row'}, dimensions={0}, use_global_device_ids=true | all-gather | bytes 147456 | tf_op jit(solution)/shard_map/all_gather | solution.py:47
  35.8 1.0 fusion.24
  36.8 10.1 %psum.105 = bf16[1,64,128]{2,1,0:T(8,128)(2,1)S(1)} all-reduce(bf16[1,64,128]{2,1,0:T(8,128)(2,1)S(1)} %fusion.24), channel_id=1, replica_groups=mesh['row'=8,'col'=4] {'col'}, use_global_device_ids=true, to_apply=%region_0.1 | all-reduce | flops 8192 | bytes 32768 | tf_op jit(solution)/shard_map/psum | solution.py:40
  47.0 1.1 bitcast_dynamic-update-slice_fusion.9
  48.1 1.0 convolution_bitcast_fusion.15
  49.1 0.2 convolution_bitcast_fusion.13
  49.4 0.2 convolution_bitcast_fusion.10
  49.6 0.2 convolution_bitcast_fusion.6
  49.8 30.7 %all-gather.1 = bf16[512,128]{1,0:T(8,128)(2,1)S(1)} all-gather(bf16[64,128]{1,0:T(8,128)(2,1)S(1)} %convert_element_type.130), channel_id=3, replica_groups=mesh['row'=8,'col'=4] {'row'}, dimensions={0}, use_global_device_ids=true | all-gather | bytes 147456 | tf_op jit(solution)/shard_map/all_gather | solution.py:47
  80.5 0.2 fusion.23
  80.7 10.1 %psum.106 = bf16[1,64,128]{2,1,0:T(8,128)(2,1)S(1)} all-reduce(bf16[1,64,128]{2,1,0:T(8,128)(2,1)S(1)} %fusion.23), channel_id=1, replica_groups=mesh['row'=8,'col'=4] {'col'}, use_global_device_ids=true, to_apply=%region_1.2 | all-reduce | flops 8192 | bytes 32768 | tf_op jit(solution)/shard_map/psum | solution.py:40
  90.8 0.2 fusion.13
  91.0 0.2 fusion.11
  91.3 0.2 fusion.8
  91.5 0.5 copy-done.2
  92.0 0.2 bitcast_dynamic-update-slice_fusion.8
  92.2 30.5 %all-gather.2 = bf16[512,128]{1,0:T(8,128)(2,1)S(1)} all-gather(bf16[64,128]{1,0:T(8,128)(2,1)S(1)} %convert_element_type.135), channel_id=4, replica_groups=mesh['row'=8,'col'=4] {'row'}, dimensions={0}, use_global_device_ids=true | all-gather | bytes 147456 | tf_op jit(solution)/shard_map/all_gather | solution.py:47
  122.8 0.2 fusion.22
  123.0 10.1 %psum.107 = bf16[1,64,128]{2,1,0:T(8,128)(2,1)S(1)} all-reduce(bf16[1,64,128]{2,1,0:T(8,128)(2,1)S(1)} %fusion.22), channel_id=1, replica_groups=mesh['row'=8,'col'=4] {'col'}, use_global_device_ids=true, to_apply=%region_2.3 | all-reduce | flops 8192 | bytes 32768 | tf_op jit(solution)/shard_map/psum | solution.py:40
  133.1 0.2 fusion.10
  133.3 0.2 fusion.7
  133.5 0.3 bitcast_dynamic-update-slice_fusion.7
  133.8 30.5 %all-gather.3 = bf16[512,128]{1,0:T(8,128)(2,1)S(1)} all-gather(bf16[64,128]{1,0:T(8,128)(2,1)S(1)} %convert_element_type.140), channel_id=5, replica_groups=mesh['row'=8,'col'=4] {'row'}, dimensions={0}, use_global_device_ids=true | all-gather | bytes 147456 | tf_op jit(solution)/shard_map/all_gather | solution.py:47
  164.3 0.2 fusion.21
  164.5 0.2 fusion.6
  164.8 10.1 %psum.108 = bf16[1,64,128]{2,1,0:T(8,128)(2,1)S(1)} all-reduce(bf16[1,64,128]{2,1,0:T(8,128)(2,1)S(1)} %fusion.21), channel_id=1, replica_groups=mesh['row'=8,'col'=4] {'col'}, use_global_device_ids=true, to_apply=%region_3.4 | all-reduce | flops 8192 | bytes 32768 | tf_op jit(solution)/shard_map/psum | solution.py:40
  174.9 0.2 bitcast_dynamic-update-slice_fusion.6
  175.2 30.5 %all-gather.4 = bf16[512,128]{1,0:T(8,128)(2,1)S(1)} all-gather(bf16[64,128]{1,0:T(8,128)(2,1)S(1)} %convert_element_type.145), channel_id=6, replica_groups=mesh['row'=8,'col'=4] {'row'}, dimensions={0}, use_global_device_ids=true | all-gather | bytes 147456 | tf_op jit(solution)/shard_map/all_gather | solution.py:47
  205.7 0.2 fusion.20
  205.9 10.1 %psum.109 = bf16[1,64,128]{2,1,0:T(8,128)(2,1)S(1)} all-reduce(bf16[1,64,128]{2,1,0:T(8,128)(2,1)S(1)} %fusion.20), channel_id=1, replica_groups=mesh['row'=8,'col'=4] {'col'}, use_global_device_ids=true, to_apply=%region_4.5 | all-reduce | flops 8192 | bytes 32768 | tf_op jit(solution)/shard_map/psum | solution.py:40
  216.0 0.2 bitcast_dynamic-update-slice_fusion.5
  216.3 0.2 fusion.297
  216.5 0.2 convolution_bitcast_fusion
  216.7 37.5 %psum.110 = bf16[2,64,128]{2,1,0:T(8,128)(2,1)S(1)} all-reduce(f32[2,64,128]{2,1,0:T(8,128)S(1)} %convolution_bitcast_fusion), channel_id=1, replica_groups=mesh['row'=8,'col'=4] {'row'}, use_global_device_ids=true, to_apply=%region_5.6 | all-reduce | flops 16384 | bytes 98304 | tf_op jit(solution)/shard_map/psum | solution.py:64
  254.2 10.1 %psum.111 = bf16[1,64,128]{2,1,0:T(8,128)(2,1)S(1)} all-reduce(bf16[1,64,128]{2,1,0:T(8,128)(2,1)S(1)} %fusion.221), channel_id=1, replica_groups=mesh['row'=8,'col'=4] {'col'}, use_global_device_ids=true, to_apply=%region_6.7 | all-reduce | flops 8192 | bytes 32768 | tf_op jit(solution)/shard_map/psum | solution.py:9
  264.3 0.2 fusion.298
  264.5 0.2 fusion.41
  264.7 0.2 fusion.3
  264.9 33.4 %psum.112 = bf16[2,64,128]{2,1,0:T(8,128)(2,1)S(1)} all-reduce(f32[2,64,128]{2,1,0:T(8,128)S(1)} %fusion.3), channel_id=1, replica_groups=mesh['row'=8,'col'=4] {'row'}, use_global_device_ids=true, to_apply=%region_7.8 | all-reduce | flops 16384 | bytes 98304 | tf_op jit(solution)/shard_map/psum | solution.py:64
  298.3 10.1 %psum.113 = bf16[1,64,128]{2,1,0:T(8,128)(2,1)S(1)} all-reduce(bf16[1,64,128]{2,1,0:T(8,128)(2,1)S(1)} %fusion.222), channel_id=1, replica_groups=mesh['row'=8,'col'=4] {'col'}, use_global_device_ids=true, to_apply=%region_8.9 | all-reduce | flops 8192 | bytes 32768 | tf_op jit(solution)/shard_map/psum | solution.py:9
  308.4 0.2 fusion.52
  308.6 0.2 fusion.38
  308.8 0.2 convolution_add_fusion.8
  309.0 0.2 fusion.2
  309.2 35.3 %psum.114 = bf16[2,64,128]{2,1,0:T(8,128)(2,1)S(1)} all-reduce(f32[2,64,128]{2,1,0:T(8,128)S(1)} %fusion.2), channel_id=1, replica_groups=mesh['row'=8,'col'=4] {'row'}, use_global_device_ids=true, to_apply=%region_9.10 | all-reduce | flops 16384 | bytes 98304 | tf_op jit(solution)/shard_map/psum | solution.py:64
  344.6 10.1 %psum.115 = bf16[1,64,128]{2,1,0:T(8,128)(2,1)S(1)} all-reduce(bf16[1,64,128]{2,1,0:T(8,128)(2,1)S(1)} %fusion.223), channel_id=1, replica_groups=mesh['row'=8,'col'=4] {'col'}, use_global_device_ids=true, to_apply=%region_10.11 | all-reduce | flops 8192 | bytes 32768 | tf_op jit(solution)/shard_map/psum | solution.py:9
  354.7 0.2 fusion.56
  354.9 0.2 fusion.34
  355.1 0.2 convolution_add_fusion.6
  355.3 0.2 convolution_add_fusion.5
  355.5 0.2 fusion.1
  355.7 33.4 %psum.116 = bf16[2,64,128]{2,1,0:T(8,128)(2,1)S(1)} all-reduce(f32[2,64,128]{2,1,0:T(8,128)S(1)} %fusion.1), channel_id=1, replica_groups=mesh['row'=8,'col'=4] {'row'}, use_global_device_ids=true, to_apply=%region_11.12 | all-reduce | flops 16384 | bytes 98304 | tf_op jit(solution)/shard_map/psum | solution.py:64
  389.1 10.1 %psum.117 = bf16[1,64,128]{2,1,0:T(8,128)(2,1)S(1)} all-reduce(bf16[1,64,128]{2,1,0:T(8,128)(2,1)S(1)} %fusion.224), channel_id=1, replica_groups=mesh['row'=8,'col'=4] {'col'}, use_global_device_ids=true, to_apply=%region_12.13 | all-reduce | flops 8192 | bytes 32768 | tf_op jit(solution)/shard_map/psum | solution.py:9
  399.2 0.2 fusion.60
  399.4 0.2 fusion.29
  399.6 0.2 convolution_add_fusion.3
  399.8 0.2 convolution_add_fusion.2
  400.0 0.2 convolution_add_fusion.1
  400.2 0.2 fusion
  400.4 35.3 %psum.118 = bf16[2,64,128]{2,1,0:T(8,128)(2,1)S(1)} all-reduce(f32[2,64,128]{2,1,0:T(8,128)S(1)} %fusion), channel_id=1, replica_groups=mesh['row'=8,'col'=4] {'row'}, use_global_device_ids=true, to_apply=%region_13.14 | all-reduce | flops 16384 | bytes 98304 | tf_op jit(solution)/shard_map/psum | solution.py:64
  435.8 10.1 %psum.119 = bf16[1,64,128]{2,1,0:T(8,128)(2,1)S(1)} all-reduce(bf16[1,64,128]{2,1,0:T(8,128)(2,1)S(1)} %fusion.225), channel_id=1, replica_groups=mesh['row'=8,'col'=4] {'col'}, use_global_device_ids=true, to_apply=%region_14.15 | all-reduce | flops 8192 | bytes 32768 | tf_op jit(solution)/shard_map/psum | solution.py:9
  446.2 0.7 copy-done.4
  (24 shorter events, 0.3 us)
Async XLA Ops:
  0.6 48.5 %copy-start = (bf16[15,1,2,128,128]{4,3,2,1,0:T(8,128)(2,1)S(1)}, bf16[15,1,2,128,128]{4,3,2,1,0:T(8,128)(2,1)}, u32[]{:S(2)}) copy-start(bf16[15,1,2,128,128]{4,3,2,1,0:T(8,128)(2,1)} %param.6) | copy-start | bytes 2949124
  49.8 41.7 %copy-start.1 = (f32[6,1,128,128]{3,2,1,0:T(8,128)S(1)}, f32[6,1,128,128]{3,2,1,0:T(8,128)}, u32[]{:S(2)}) copy-start(f32[6,1,128,128]{3,2,1,0:T(8,128)} %param.5) | copy-start | bytes 1179652
  91.0 1.0 copy-start.2
  216.3 37.9 %copy-start.3 = (f32[6,1,64,128]{3,2,1,0:T(8,128)}, f32[6,1,64,128]{3,2,1,0:T(8,128)S(1)}, u32[]{:S(2)}) copy-start(f32[6,1,64,128]{3,2,1,0:T(8,128)S(1)} %get-tuple-element.27) | copy-start | bytes 589828
  446.1 0.7 copy-start.4
where the time goes:
time: 448 us; the launch traced here: 447 us
  blocking collectives  431 us (96%)
  matrix products  12.2 us (3%)
    psum x5, blocking collectives, shards(): summed = lax.psum(partial_value, 'row')  175 us
    all_gather x5, blocking collectives, shards(): lax.all_gather(segment.astype(jnp.bfloat16), 'row', axis=0, tiled=True)  155 us
    psum x5, blocking collectives, shards(): lax.psum(partial_value.astype(jnp.bfloat16), 'col').astype(jnp.float32)  50.7 us
    psum x5, blocking collectives, spread(): return lax.psum(block, axis)  50.6 us

commit v1 on v0

--- a/solution.py
+++ b/solution.py
@@ -44,7 +44,19 @@
         )
         solved.append(segment)
         if height < levels - 1:
-            gathered_all = lax.all_gather(segment.astype(jnp.bfloat16), "row", axis=0, tiled=True)
+            x = segment.astype(jnp.bfloat16)
+            ways, here, step = (lax.axis_size("row"), lax.axis_index("row"), x.shape[0])
+            line, have = (x, 1)
+            while have < ways:
+                line = jnp.concatenate(
+                    [
+                        line,
+                        lax.ppermute(line, "row", [(d, (d - have) % ways) for d in range(ways)]),
+                    ],
+                    axis=0,
+                )
+                have = 2 * have
+            gathered_all = jnp.roll(line, here * step, axis=0)
             gathered.append(
                 lax.dynamic_slice_in_dim(gathered_all, col_index * width_col, width_col, 0)
             )

time: 448 us -> 378 us (0.84)
  blocking collectives: 431 us -> 278 us
  waiting for transfers between devices: 0 us -> 47.3 us
  starting transfers between devices: 0 us -> 36.6 us
    all_gather x5 -> x0, blocking collectives: 155 us -> none  [shards(): lax.all_gather(segment.astype(jnp.bfloat16), 'row', axis=0, tiled=True)]
    ppermute x0 -> x15, waiting for transfers between devices: none -> 47.3 us  [shards(): lax.ppermute(line, 'row', [(d, (d - have) % ways) for d in range(ways)])]
    ppermute x0 -> x15, starting transfers between devices: none -> 36.6 us  [shards(): lax.ppermute(line, 'row', [(d, (d - have) % ways) for d in range(ways)])]
  transfers between devices with their start and end apart: 0 -> 15, of which waited for: 0 -> 15; matrix products, arithmetic and copies ran while one was open for 0% -> 1% of each run, Pallas kernels for 0% -> 0%
where the time goes in v1:
time: 378 us; the launch traced here: 377 us
  blocking collectives  278 us (74%)
  waiting for transfers between devices  47.3 us (13%)
  starting transfers between devices  36.6 us (10%)
  matrix products  11.3 us (3%)
    psum x5, blocking collectives, shards(): summed = lax.psum(partial_value, 'row')  177 us
    psum x5, blocking collectives, shards(): lax.psum(partial_value.astype(jnp.bfloat16), 'col').astype(jnp.float32)  50.7 us
    psum x5, blocking collectives, spread(): return lax.psum(block, axis)  50.6 us
    ppermute x15, waiting for transfers between devices, shards(): lax.ppermute(line, 'row', [(d, (d - have) % ways) for d in range(ways)])  47.3 us
    ppermute x15, starting transfers between devices, shards(): lax.ppermute(line, 'row', [(d, (d - have) % ways) for d in range(ways)])  36.6 us
  transfers between devices with their start and end apart: 15, of which 15 were waited for; matrix products, arithmetic and copies ran while one was open for 1% of the time, Pallas kernels for 0%

profile of v1, /device:TPU:0, one launch (start us, length us, event | category | flops | bytes accessed | tf_op | source)
XLA Modules:
  0.0 377.2 jit_solution(11090567173601093742)
XLA Ops:
  0.6 1.2 bitcast_dynamic-update-slice_fusion.10
  1.8 6.1 %collective-permute-start = (bf16[1,64,128]{2,1,0:T(8,128)(2,1)S(1)}, bf16[1,64,128]{2,1,0:T(8,128)(2,1)S(1)}, u32[]{:S(2)}, u32[]{:S(2)}) collective-permute-start(bf16[1,64,128]{2,1,0:T(8,128)(2,1)S(1)} %convert_bitcast_fusion.4), channel_id=1, source_target_pairs={{0,28},{4,0},{8,4},{12,8},{16,12},{20,16},{24,20},{28,24},{1,29},{... | collective-permute-start | bytes 49160 | tf_op jit(solution)/shard_map/ppermute | solution.py:54
  7.9 1.4 collective-permute-done
  9.3 1.4 collective-permute-start.1
  10.7 2.5 collective-permute-done.1
  13.3 0.4 collective-permute-start.2
  13.7 1.7 compare_reduce_fusion
  15.4 3.8 %collective-permute-done.2 = bf16[4,64,128]{2,1,0:T(8,128)(2,1)S(1)} collective-permute-done((bf16[4,64,128]{2,1,0:T(8,128)(2,1)S(1)}, bf16[4,64,128]{2,1,0:T(8,128)(2,1)S(1)}, u32[]{:S(2)}, u32[]{:S(2)}) %collective-permute-start.2) | collective-permute-done | bytes 65568 | tf_op jit(solution)/shard_map/ppermute | solution.py:54
  19.3 1.0 fusion.24
  20.3 10.1 %psum.105 = bf16[1,64,128]{2,1,0:T(8,128)(2,1)S(1)} all-reduce(bf16[1,64,128]{2,1,0:T(8,128)(2,1)S(1)} %fusion.24), channel_id=1, replica_groups=mesh['row'=8,'col'=4] {'col'}, use_global_device_ids=true, to_apply=%region_0.2 | all-reduce | flops 8192 | bytes 32768 | tf_op jit(solution)/shard_map/psum | solution.py:40
  30.5 1.1 bitcast_dynamic-update-slice_fusion.9
  31.6 6.2 %collective-permute-start.3 = (bf16[1,64,128]{2,1,0:T(8,128)(2,1)S(1)}, bf16[1,64,128]{2,1,0:T(8,128)(2,1)S(1)}, u32[]{:S(2)}, u32[]{:S(2)}) collective-permute-start(bf16[1,64,128]{2,1,0:T(8,128)(2,1)S(1)} %convert_bitcast_fusion.3), channel_id=1, source_target_pairs={{0,28},{4,0},{8,4},{12,8},{16,12},{20,16},{24,20},{28,24},{1,29},{... | collective-permute-start | bytes 49160 | tf_op jit(solution)/shard_map/ppermute | solution.py:54
  37.8 1.4 collective-permute-done.3
  39.3 0.8 collective-permute-start.4
  40.1 3.1 collective-permute-done.4
  43.5 5.6 %collective-permute-done.5 = bf16[4,64,128]{2,1,0:T(8,128)(2,1)S(1)} collective-permute-done((bf16[4,64,128]{2,1,0:T(8,128)(2,1)S(1)}, bf16[4,64,128]{2,1,0:T(8,128)(2,1)S(1)}, u32[]{:S(2)}, u32[]{:S(2)}) %collective-permute-start.5) | collective-permute-done | bytes 65568 | tf_op jit(solution)/shard_map/ppermute | solution.py:54
  49.2 0.2 fusion.23
  49.4 10.1 %psum.106 = bf16[1,64,128]{2,1,0:T(8,128)(2,1)S(1)} all-reduce(bf16[1,64,128]{2,1,0:T(8,128)(2,1)S(1)} %fusion.23), channel_id=1, replica_groups=mesh['row'=8,'col'=4] {'col'}, use_global_device_ids=true, to_apply=%region_1.3 | all-reduce | flops 8192 | bytes 32768 | tf_op jit(solution)/shard_map/psum | solution.py:40
  59.5 0.2 bitcast_dynamic-update-slice_fusion.8
  59.8 6.3 %collective-permute-start.6 = (bf16[1,64,128]{2,1,0:T(8,128)(2,1)S(1)}, bf16[1,64,128]{2,1,0:T(8,128)(2,1)S(1)}, u32[]{:S(2)}, u32[]{:S(2)}) collective-permute-start(bf16[1,64,128]{2,1,0:T(8,128)(2,1)S(1)} %convert_bitcast_fusion.2), channel_id=1, source_target_pairs={{0,28},{4,0},{8,4},{12,8},{16,12},{20,16},{24,20},{28,24},{1,29},{... | collective-permute-start | bytes 49160 | tf_op jit(solution)/shard_map/ppermute | solution.py:54
  66.3 1.2 collective-permute-done.6
  67.5 0.8 collective-permute-start.7
  68.6 2.9 collective-permute-done.7
  71.8 5.7 %collective-permute-done.8 = bf16[4,64,128]{2,1,0:T(8,128)(2,1)S(1)} collective-permute-done((bf16[4,64,128]{2,1,0:T(8,128)(2,1)S(1)}, bf16[4,64,128]{2,1,0:T(8,128)(2,1)S(1)}, u32[]{:S(2)}, u32[]{:S(2)}) %collective-permute-start.8) | collective-permute-done | bytes 65568 | tf_op jit(solution)/shard_map/ppermute | solution.py:54
  77.5 0.2 fusion.22
  77.7 10.1 %psum.107 = bf16[1,64,128]{2,1,0:T(8,128)(2,1)S(1)} all-reduce(bf16[1,64,128]{2,1,0:T(8,128)(2,1)S(1)} %fusion.22), channel_id=1, replica_groups=mesh['row'=8,'col'=4] {'col'}, use_global_device_ids=true, to_apply=%region_2.4 | all-reduce | flops 8192 | bytes 32768 | tf_op jit(solution)/shard_map/psum | solution.py:40
  87.8 0.2 bitcast_dynamic-update-slice_fusion.7
  88.1 6.3 %collective-permute-start.9 = (bf16[1,64,128]{2,1,0:T(8,128)(2,1)S(1)}, bf16[1,64,128]{2,1,0:T(8,128)(2,1)S(1)}, u32[]{:S(2)}, u32[]{:S(2)}) collective-permute-start(bf16[1,64,128]{2,1,0:T(8,128)(2,1)S(1)} %convert_bitcast_fusion.1), channel_id=1, source_target_pairs={{0,28},{4,0},{8,4},{12,8},{16,12},{20,16},{24,20},{28,24},{1,29},{... | collective-permute-start | bytes 49160 | tf_op jit(solution)/shard_map/ppermute | solution.py:54
  94.6 1.2 collective-permute-done.9
  95.8 0.8 collective-permute-start.10
  96.9 2.9 collective-permute-done.10
  100.0 5.7 %collective-permute-done.11 = bf16[4,64,128]{2,1,0:T(8,128)(2,1)S(1)} collective-permute-done((bf16[4,64,128]{2,1,0:T(8,128)(2,1)S(1)}, bf16[4,64,128]{2,1,0:T(8,128)(2,1)S(1)}, u32[]{:S(2)}, u32[]{:S(2)}) %collective-permute-start.11) | collective-permute-done | bytes 65568 | tf_op jit(solution)/shard_map/ppermute | solution.py:54
  105.8 0.2 fusion.21
  106.0 10.1 %psum.108 = bf16[1,64,128]{2,1,0:T(8,128)(2,1)S(1)} all-reduce(bf16[1,64,128]{2,1,0:T(8,128)(2,1)S(1)} %fusion.21), channel_id=1, replica_groups=mesh['row'=8,'col'=4] {'col'}, use_global_device_ids=true, to_apply=%region_3.5 | all-reduce | flops 8192 | bytes 32768 | tf_op jit(solution)/shard_map/psum | solution.py:40
  116.1 0.2 bitcast_dynamic-update-slice_fusion.6
  116.4 6.3 %collective-permute-start.12 = (bf16[1,64,128]{2,1,0:T(8,128)(2,1)S(1)}, bf16[1,64,128]{2,1,0:T(8,128)(2,1)S(1)}, u32[]{:S(2)}, u32[]{:S(2)}) collective-permute-start(bf16[1,64,128]{2,1,0:T(8,128)(2,1)S(1)} %convert_bitcast_fusion), channel_id=1, source_target_pairs={{0,28},{4,0},{8,4},{12,8},{16,12},{20,16},{24,20},{28,24},{1,29},{... | collective-permute-start | bytes 49160 | tf_op jit(solution)/shard_map/ppermute | solution.py:54
  122.9 1.2 collective-permute-done.12
  124.1 0.8 collective-permute-start.13
  125.2 2.9 collective-permute-done.13
  128.3 5.7 %collective-permute-done.14 = bf16[4,64,128]{2,1,0:T(8,128)(2,1)S(1)} collective-permute-done((bf16[4,64,128]{2,1,0:T(8,128)(2,1)S(1)}, bf16[4,64,128]{2,1,0:T(8,128)(2,1)S(1)}, u32[]{:S(2)}, u32[]{:S(2)}) %collective-permute-start.14) | collective-permute-done | bytes 65568 | tf_op jit(solution)/shard_map/ppermute | solution.py:54
  134.0 0.2 fusion.20
  134.2 10.1 %psum.109 = bf16[1,64,128]{2,1,0:T(8,128)(2,1)S(1)} all-reduce(bf16[1,64,128]{2,1,0:T(8,128)(2,1)S(1)} %fusion.20), channel_id=1, replica_groups=mesh['row'=8,'col'=4] {'col'}, use_global_device_ids=true, to_apply=%region_4.6 | all-reduce | flops 8192 | bytes 32768 | tf_op jit(solution)/shard_map/psum | solution.py:40
  144.3 0.2 bitcast_dynamic-update-slice_fusion.5
  145.0 39.6 %psum.110 = bf16[2,64,128]{2,1,0:T(8,128)(2,1)S(1)} all-reduce(f32[2,64,128]{2,1,0:T(8,128)S(1)} %convolution_bitcast_fusion), channel_id=1, replica_groups=mesh['row'=8,'col'=4] {'row'}, use_global_device_ids=true, to_apply=%region_5.7 | all-reduce | flops 16384 | bytes 98304 | tf_op jit(solution)/shard_map/psum | solution.py:76
  184.5 10.1 %psum.111 = bf16[1,64,128]{2,1,0:T(8,128)(2,1)S(1)} all-reduce(bf16[1,64,128]{2,1,0:T(8,128)(2,1)S(1)} %fusion.252), channel_id=1, replica_groups=mesh['row'=8,'col'=4] {'col'}, use_global_device_ids=true, to_apply=%region_6.8 | all-reduce | flops 8192 | bytes 32768 | tf_op jit(solution)/shard_map/psum | solution.py:9
  195.1 0.2 fusion.3
  195.3 33.4 %psum.112 = bf16[2,64,128]{2,1,0:T(8,128)(2,1)S(1)} all-reduce(f32[2,64,128]{2,1,0:T(8,128)S(1)} %fusion.3), channel_id=1, replica_groups=mesh['row'=8,'col'=4] {'row'}, use_global_device_ids=true, to_apply=%region_7.9 | all-reduce | flops 16384 | bytes 98304 | tf_op jit(solution)/shard_map/psum | solution.py:76
  228.7 10.1 %psum.113 = bf16[1,64,128]{2,1,0:T(8,128)(2,1)S(1)} all-reduce(bf16[1,64,128]{2,1,0:T(8,128)(2,1)S(1)} %fusion.253), channel_id=1, replica_groups=mesh['row'=8,'col'=4] {'col'}, use_global_device_ids=true, to_apply=%region_8.10 | all-reduce | flops 8192 | bytes 32768 | tf_op jit(solution)/shard_map/psum | solution.py:9
  239.2 0.2 convolution_add_fusion.8
  239.4 0.2 fusion.2
  239.6 35.3 %psum.114 = bf16[2,64,128]{2,1,0:T(8,128)(2,1)S(1)} all-reduce(f32[2,64,128]{2,1,0:T(8,128)S(1)} %fusion.2), channel_id=1, replica_groups=mesh['row'=8,'col'=4] {'row'}, use_global_device_ids=true, to_apply=%region_9.11 | all-reduce | flops 16384 | bytes 98304 | tf_op jit(solution)/shard_map/psum | solution.py:76
  274.9 10.1 %psum.115 = bf16[1,64,128]{2,1,0:T(8,128)(2,1)S(1)} all-reduce(bf16[1,64,128]{2,1,0:T(8,128)(2,1)S(1)} %fusion.254), channel_id=1, replica_groups=mesh['row'=8,'col'=4] {'col'}, use_global_device_ids=true, to_apply=%region_10.12 | all-reduce | flops 8192 | bytes 32768 | tf_op jit(solution)/shard_map/psum | solution.py:9
  285.4 0.2 convolution_add_fusion.6
  285.6 0.2 convolution_add_fusion.5
  285.8 0.2 fusion.1
  286.1 33.4 %psum.116 = bf16[2,64,128]{2,1,0:T(8,128)(2,1)S(1)} all-reduce(f32[2,64,128]{2,1,0:T(8,128)S(1)} %fusion.1), channel_id=1, replica_groups=mesh['row'=8,'col'=4] {'row'}, use_global_device_ids=true, to_apply=%region_11.13 | all-reduce | flops 16384 | bytes 98304 | tf_op jit(solution)/shard_map/psum | solution.py:76
  319.5 10.1 %psum.117 = bf16[1,64,128]{2,1,0:T(8,128)(2,1)S(1)} all-reduce(bf16[1,64,128]{2,1,0:T(8,128)(2,1)S(1)} %fusion.255), channel_id=1, replica_groups=mesh['row'=8,'col'=4] {'col'}, use_global_device_ids=true, to_apply=%region_12.14 | all-reduce | flops 8192 | bytes 32768 | tf_op jit(solution)/shard_map/psum | solution.py:9
  330.0 0.2 convolution_add_fusion.3
  330.2 0.2 convolution_add_fusion.2
  330.4 0.2 convolution_add_fusion.1
  330.6 0.2 fusion
  330.8 35.3 %psum.118 = bf16[2,64,128]{2,1,0:T(8,128)(2,1)S(1)} all-reduce(f32[2,64,128]{2,1,0:T(8,128)S(1)} %fusion), channel_id=1, replica_groups=mesh['row'=8,'col'=4] {'row'}, use_global_device_ids=true, to_apply=%region_13.15 | all-reduce | flops 16384 | bytes 98304 | tf_op jit(solution)/shard_map/psum | solution.py:76
  366.1 10.1 %psum.119 = bf16[1,64,128]{2,1,0:T(8,128)(2,1)S(1)} all-reduce(bf16[1,64,128]{2,1,0:T(8,128)(2,1)S(1)} %fusion.256), channel_id=1, replica_groups=mesh['row'=8,'col'=4] {'col'}, use_global_device_ids=true, to_apply=%region_14.16 | all-reduce | flops 8192 | bytes 32768 | tf_op jit(solution)/shard_map/psum | solution.py:9
  376.5 0.7 copy-done.4
  (63 shorter events, 4.8 us)
Async XLA Ops:
  0.6 42.6 %copy-start = (bf16[15,1,2,128,128]{4,3,2,1,0:T(8,128)(2,1)S(1)}, bf16[15,1,2,128,128]{4,3,2,1,0:T(8,128)(2,1)}, u32[]{:S(2)}) copy-start(bf16[15,1,2,128,128]{4,3,2,1,0:T(8,128)(2,1)} %param.8) | copy-start | bytes 2949124
  1.8 7.5 %collective-permute-start = (bf16[1,64,128]{2,1,0:T(8,128)(2,1)S(1)}, bf16[1,64,128]{2,1,0:T(8,128)(2,1)S(1)}, u32[]{:S(2)}, u32[]{:S(2)}) collective-permute-start(bf16[1,64,128]{2,1,0:T(8,128)(2,1)S(1)} %convert_bitcast_fusion.4), channel_id=1, source_target_pairs={{0,28},{4,0},{8,4},{12,8},{16,12},{20,16},{24,20},{28,24},{1,29},{... | collective-permute-start | bytes 49160 | tf_op jit(solution)/shard_map/ppermute | solution.py:54
  9.3 3.9 %collective-permute-start.1 = (bf16[2,64,128]{2,1,0:T(8,128)(2,1)S(1)}, bf16[2,64,128]{2,1,0:T(8,128)(2,1)S(1)}, u32[]{:S(2)}, u32[]{:S(2)}) collective-permute-start(bf16[2,64,128]{2,1,0:T(8,128)(2,1)S(1)} %pad_maximum_fusion.5), channel_id=1, source_target_pairs={{0,24},{4,28},{8,0},{12,4},{16,8},{20,12},{24,16},{28,20},{1,25},{... | collective-permute-start | bytes 98312 | tf_op jit(solution)/shard_map/ppermute | solution.py:54
  13.3 5.9 %collective-permute-start.2 = (bf16[4,64,128]{2,1,0:T(8,128)(2,1)S(1)}, bf16[4,64,128]{2,1,0:T(8,128)(2,1)S(1)}, u32[]{:S(2)}, u32[]{:S(2)}) collective-permute-start(bf16[4,64,128]{2,1,0:T(8,128)(2,1)S(1)} %pad_maximum_fusion), channel_id=1, source_target_pairs={{0,16},{4,20},{8,24},{12,28},{16,0},{20,4},{24,8},{28,12},{1,17},{... | collective-permute-start | bytes 196616 | tf_op jit(solution)/shard_map/ppermute | solution.py:54
  31.6 28.0 %copy-start.1 = (f32[6,1,128,128]{3,2,1,0:T(8,128)S(1)}, f32[6,1,128,128]{3,2,1,0:T(8,128)}, u32[]{:S(2)}) copy-start(f32[6,1,128,128]{3,2,1,0:T(8,128)} %param.7) | copy-start | bytes 1179652
  31.6 7.7 %collective-permute-start.3 = (bf16[1,64,128]{2,1,0:T(8,128)(2,1)S(1)}, bf16[1,64,128]{2,1,0:T(8,128)(2,1)S(1)}, u32[]{:S(2)}, u32[]{:S(2)}) collective-permute-start(bf16[1,64,128]{2,1,0:T(8,128)(2,1)S(1)} %convert_bitcast_fusion.3), channel_id=1, source_target_pairs={{0,28},{4,0},{8,4},{12,8},{16,12},{20,16},{24,20},{28,24},{1,29},{... | collective-permute-start | bytes 49160 | tf_op jit(solution)/shard_map/ppermute | solution.py:54
  39.3 3.9 %collective-permute-start.4 = (bf16[2,64,128]{2,1,0:T(8,128)(2,1)S(1)}, bf16[2,64,128]{2,1,0:T(8,128)(2,1)S(1)}, u32[]{:S(2)}, u32[]{:S(2)}) collective-permute-start(bf16[2,64,128]{2,1,0:T(8,128)(2,1)S(1)} %pad_maximum_fusion.6), channel_id=1, source_target_pairs={{0,24},{4,28},{8,0},{12,4},{16,8},{20,12},{24,16},{28,20},{1,25},{... | collective-permute-start | bytes 98312 | tf_op jit(solution)/shard_map/ppermute | solution.py:54
  43.2 5.9 %collective-permute-start.5 = (bf16[4,64,128]{2,1,0:T(8,128)(2,1)S(1)}, bf16[4,64,128]{2,1,0:T(8,128)(2,1)S(1)}, u32[]{:S(2)}, u32[]{:S(2)}) collective-permute-start(bf16[4,64,128]{2,1,0:T(8,128)(2,1)S(1)} %pad_maximum_fusion.1), channel_id=1, source_target_pairs={{0,16},{4,20},{8,24},{12,28},{16,0},{20,4},{24,8},{28,12},{1,17},{... | collective-permute-start | bytes 196616 | tf_op jit(solution)/shard_map/ppermute | solution.py:54
  43.5 16.1 %copy-start.2 = (f32[6,1,64,128]{3,2,1,0:T(8,128)S(1)}, f32[6,1,64,128]{3,2,1,0:T(8,128)}, u32[]{:S(2)}) copy-start(f32[6,1,64,128]{3,2,1,0:T(8,128)} %param.6) | copy-start | bytes 589828
  59.8 7.8 %collective-permute-start.6 = (bf16[1,64,128]{2,1,0:T(8,128)(2,1)S(1)}, bf16[1,64,128]{2,1,0:T(8,128)(2,1)S(1)}, u32[]{:S(2)}, u32[]{:S(2)}) collective-permute-start(bf16[1,64,128]{2,1,0:T(8,128)(2,1)S(1)} %convert_bitcast_fusion.2), channel_id=1, source_target_pairs={{0,28},{4,0},{8,4},{12,8},{16,12},{20,16},{24,20},{28,24},{1,29},{... | collective-permute-start | bytes 49160 | tf_op jit(solution)/shard_map/ppermute | solution.py:54
  67.5 3.9 %collective-permute-start.7 = (bf16[2,64,128]{2,1,0:T(8,128)(2,1)S(1)}, bf16[2,64,128]{2,1,0:T(8,128)(2,1)S(1)}, u32[]{:S(2)}, u32[]{:S(2)}) collective-permute-start(bf16[2,64,128]{2,1,0:T(8,128)(2,1)S(1)} %pad_maximum_fusion.7), channel_id=1, source_target_pairs={{0,24},{4,28},{8,0},{12,4},{16,8},{20,12},{24,16},{28,20},{1,25},{... | collective-permute-start | bytes 98312 | tf_op jit(solution)/shard_map/ppermute | solution.py:54
  71.5 5.9 %collective-permute-start.8 = (bf16[4,64,128]{2,1,0:T(8,128)(2,1)S(1)}, bf16[4,64,128]{2,1,0:T(8,128)(2,1)S(1)}, u32[]{:S(2)}, u32[]{:S(2)}) collective-permute-start(bf16[4,64,128]{2,1,0:T(8,128)(2,1)S(1)} %pad_maximum_fusion.2), channel_id=1, source_target_pairs={{0,16},{4,20},{8,24},{12,28},{16,0},{20,4},{24,8},{28,12},{1,17},{... | collective-permute-start | bytes 196616 | tf_op jit(solution)/shard_map/ppermute | solution.py:54
  88.1 7.8 %collective-permute-start.9 = (bf16[1,64,128]{2,1,0:T(8,128)(2,1)S(1)}, bf16[1,64,128]{2,1,0:T(8,128)(2,1)S(1)}, u32[]{:S(2)}, u32[]{:S(2)}) collective-permute-start(bf16[1,64,128]{2,1,0:T(8,128)(2,1)S(1)} %convert_bitcast_fusion.1), channel_id=1, source_target_pairs={{0,28},{4,0},{8,4},{12,8},{16,12},{20,16},{24,20},{28,24},{1,29},{... | collective-permute-start | bytes 49160 | tf_op jit(solution)/shard_map/ppermute | solution.py:54
  95.8 3.9 %collective-permute-start.10 = (bf16[2,64,128]{2,1,0:T(8,128)(2,1)S(1)}, bf16[2,64,128]{2,1,0:T(8,128)(2,1)S(1)}, u32[]{:S(2)}, u32[]{:S(2)}) collective-permute-start(bf16[2,64,128]{2,1,0:T(8,128)(2,1)S(1)} %pad_maximum_fusion.8), channel_id=1, source_target_pairs={{0,24},{4,28},{8,0},{12,4},{16,8},{20,12},{24,16},{28,20},{1,25},{... | collective-permute-start | bytes 98312 | tf_op jit(solution)/shard_map/ppermute | solution.py:54
  99.8 5.9 %collective-permute-start.11 = (bf16[4,64,128]{2,1,0:T(8,128)(2,1)S(1)}, bf16[4,64,128]{2,1,0:T(8,128)(2,1)S(1)}, u32[]{:S(2)}, u32[]{:S(2)}) collective-permute-start(bf16[4,64,128]{2,1,0:T(8,128)(2,1)S(1)} %pad_maximum_fusion.3), channel_id=1, source_target_pairs={{0,16},{4,20},{8,24},{12,28},{16,0},{20,4},{24,8},{28,12},{1,17},{... | collective-permute-start | bytes 196616 | tf_op jit(solution)/shard_map/ppermute | solution.py:54
  116.4 7.8 %collective-permute-start.12 = (bf16[1,64,128]{2,1,0:T(8,128)(2,1)S(1)}, bf16[1,64,128]{2,1,0:T(8,128)(2,1)S(1)}, u32[]{:S(2)}, u32[]{:S(2)}) collective-permute-start(bf16[1,64,128]{2,1,0:T(8,128)(2,1)S(1)} %convert_bitcast_fusion), channel_id=1, source_target_pairs={{0,28},{4,0},{8,4},{12,8},{16,12},{20,16},{24,20},{28,24},{1,29},{... | collective-permute-start | bytes 49160 | tf_op jit(solution)/shard_map/ppermute | solution.py:54
  124.1 3.9 %collective-permute-start.13 = (bf16[2,64,128]{2,1,0:T(8,128)(2,1)S(1)}, bf16[2,64,128]{2,1,0:T(8,128)(2,1)S(1)}, u32[]{:S(2)}, u32[]{:S(2)}) collective-permute-start(bf16[2,64,128]{2,1,0:T(8,128)(2,1)S(1)} %pad_maximum_fusion.9), channel_id=1, source_target_pairs={{0,24},{4,28},{8,0},{12,4},{16,8},{20,12},{24,16},{28,20},{1,25},{... | collective-permute-start | bytes 98312 | tf_op jit(solution)/shard_map/ppermute | solution.py:54
  128.0 5.9 %collective-permute-start.14 = (bf16[4,64,128]{2,1,0:T(8,128)(2,1)S(1)}, bf16[4,64,128]{2,1,0:T(8,128)(2,1)S(1)}, u32[]{:S(2)}, u32[]{:S(2)}) collective-permute-start(bf16[4,64,128]{2,1,0:T(8,128)(2,1)S(1)} %pad_maximum_fusion.4), channel_id=1, source_target_pairs={{0,16},{4,20},{8,24},{12,28},{16,0},{20,4},{24,8},{28,12},{1,17},{... | collective-permute-start | bytes 196616 | tf_op jit(solution)/shard_map/ppermute | solution.py:54
  144.6 40.0 %copy-start.3 = (f32[6,1,64,128]{3,2,1,0:T(8,128)}, f32[6,1,64,128]{3,2,1,0:T(8,128)S(1)}, u32[]{:S(2)}) copy-start(f32[6,1,64,128]{3,2,1,0:T(8,128)S(1)} %get-tuple-element.28) | copy-start | bytes 589828
  376.5 0.7 copy-start.4
